TPU v7x, 256 devices: a whole 4x4x8 slice. The times are simulated.
256 devices in a mesh: ctx: 64 (over x, y_lo, z), rep: 4 (over y_hi, core).
Axes of the slice: x: 4, y: 4 (y_hi: 2, y_lo: 2; y = y_hi * 2 + y_lo), z: 8, core: 2. Of those that a mesh axis runs over, the one named last changes fastest.
Arguments:
- tokens: bfloat16 [4, 8192, 2880], P('rep', 'ctx'), may hold values from -6 to 6
- router_w: bfloat16 [2880, 32], replicated, may hold values from -0.109375 to 0.109375
- router_b: float32 [32], replicated, may hold values from -4 to 4
- hidden: bfloat16 [4, 8192, 4, 1536], P('rep', 'ctx'), may hold values from -6 to 6
- teacher_idx: int32 [4, 8192, 4], P('rep', 'ctx'), may hold values from 0 to 31, all different within a row
- merge_map: int32 [32], replicated, may hold values from 0 to 15, as said below
- merge_coef: float32 [32], replicated, may hold values from 0.3 to 1.5
- source_w: bfloat16 [32, 1536, 1536], P(None, 'ctx'), may hold values from -0.15625 to 0.15625
- out_grad: bfloat16 [4, 8192, 1536], P('rep', 'ctx'), may hold values from -6 to 6
Outputs:
- mixed: bfloat16 [4, 8192, 1536], P('rep', 'ctx')
- hidden_grad: bfloat16 [4, 8192, 4, 1536], P('rep', 'ctx')
- token_grad: bfloat16 [4, 8192, 2880], P('rep', 'ctx')
- router_w_grad: float32 [2880, 32], replicated
- router_b_grad: float32 [32], replicated
- coef_grad: float32 [32], replicated
- source_w_grad: float32 [32, 1536, 1536], P(None, 'ctx', 'rep')
Inputs may be any that keep to these rules, and one draw needn't show every extreme that they name: `teacher_idx`: each token names 4 different experts. `merge_map`: each of the 16 combinations takes exactly two of the 32 experts.
All inputs are finite; a program needn't handle non-finite values.
Results may differ from a plain program's by a relative error of at most 0.0064.
Values may be sent and summed in bfloat16 or wider, within the bound.
A program may use at most 128 MiB of HBM per device.

v0:
```python
import math
import jax
import jax.numpy as jnp
from jax import lax
from jax.sharding import PartitionSpec as P

MERGED = 16


def expert_rows(rows_hidden, rows_grad, rows_member, lane_weights):
    row_count = rows_hidden.shape[0]
    out_rows = jnp.zeros((row_count, lane_weights.shape[1]), jnp.float32)
    back_rows = jnp.zeros((row_count, lane_weights.shape[2]), jnp.float32)
    weight = lane_weights[0]
    selected = (rows_member == 0)[:, None]
    forward = lax.dot_general(
        rows_hidden, weight, (((1,), (1,)), ((), ())), preferred_element_type=jnp.float32
    )
    out_rows = jnp.where(selected, forward, out_rows)
    backward = jnp.dot(rows_grad, weight, preferred_element_type=jnp.float32)
    back_rows = jnp.where(selected, backward, back_rows)
    masked = jnp.where(selected, rows_grad, jnp.zeros_like(rows_grad))
    grad_list = [
        lax.dot_general(
            masked, rows_hidden, (((0,), (0,)), ((), ())), preferred_element_type=jnp.float32
        )
    ]
    return (out_rows, back_rows, jnp.stack(grad_list))


def on_device(
    tokens, router_w, router_b, hidden, teacher_idx, merge_map, merge_coef, source_w, out_grad
):
    ctx_count = lax.axis_size("ctx")
    rep_count = lax.axis_size("rep")
    tok_count = tokens.shape[1]
    feature_count = tokens.shape[2]
    top_count = teacher_idx.shape[2]
    hidden_width = hidden.shape[3]
    out_width = out_grad.shape[2]
    source_count = router_w.shape[1]
    row_share = source_w.shape[1]
    per_lane = max(1, MERGED // ctx_count)
    copies = max(1, ctx_count // MERGED)
    capacity = 5 * tok_count * top_count // (4 * ctx_count)
    slot_count = tok_count * top_count
    grad_scale = 1.0 / math.sqrt(tok_count * ctx_count * rep_count)
    flat_x = tokens.reshape(tok_count, feature_count)
    logits = jnp.dot(flat_x, router_w, preferred_element_type=jnp.float32) + router_b
    choice_ids = teacher_idx.reshape(tok_count, top_count)
    pick_table = choice_ids[:, :, None] == jnp.arange(source_count, dtype=jnp.int32)[None, None, :]
    pick_float = pick_table.astype(jnp.float32)
    chosen = jnp.sum(pick_float * logits[:, None, :], axis=2)
    raised = jnp.exp(chosen)
    gate_probs = raised / jnp.sum(raised, axis=1, keepdims=True)
    merged_id = jnp.sum(jnp.where(pick_table, merge_map[None, None, :], 0), axis=2)
    position = lax.axis_index("ctx") * tok_count + jnp.arange(tok_count, dtype=jnp.int32)
    lane_id = merged_id // per_lane * copies + (position % copies)[:, None]
    member_id = (merged_id % per_lane).reshape(-1)
    lane_flat = lane_id.reshape(-1)
    onehot = (lane_flat[:, None] == jnp.arange(ctx_count, dtype=jnp.int32)[None, :]).astype(
        jnp.int32
    )
    before = jnp.cumsum(onehot, axis=0) - onehot
    slot_rank = jnp.sum(before * onehot, axis=1)
    is_kept = slot_rank < capacity
    slot_index = jnp.where(is_kept, lane_flat * capacity + slot_rank, ctx_count * capacity)
    slot_source = (
        jnp.full((ctx_count * capacity + 1,), slot_count, jnp.int32)
        .at[slot_index]
        .set(jnp.arange(slot_count, dtype=jnp.int32))[: ctx_count * capacity]
    )
    slot_grad = (gate_probs[:, :, None] * out_grad.reshape(tok_count, 1, out_width)).astype(
        jnp.bfloat16
    )
    pad_hidden = jnp.concatenate(
        [hidden.reshape(slot_count, hidden_width), jnp.zeros((1, hidden_width), jnp.bfloat16)],
        axis=0,
    )
    pad_grad = jnp.concatenate(
        [slot_grad.reshape(slot_count, out_width), jnp.zeros((1, out_width), jnp.bfloat16)], axis=0
    )
    pad_member = jnp.concatenate([member_id, jnp.zeros((1,), jnp.int32)], axis=0)
    send_hidden = pad_hidden[slot_source].reshape(ctx_count, capacity, hidden_width)
    send_grad = pad_grad[slot_source].reshape(ctx_count, capacity, out_width)
    send_member = pad_member[slot_source].reshape(ctx_count, capacity)
    lane_group = lax.axis_index("ctx") // copies
    same_group = merge_map[:, None] == merge_map[None, :]
    earlier = jnp.arange(source_count)[:, None] > jnp.arange(source_count)[None, :]
    member_rank = jnp.sum((same_group & earlier).astype(jnp.int32), axis=1)
    source_order = (
        jnp.zeros((source_count,), jnp.int32)
        .at[2 * merge_map + member_rank]
        .set(jnp.arange(source_count, dtype=jnp.int32))
    )
    picked = source_w[source_order].reshape(
        MERGED // per_lane, 2 * per_lane, row_share, hidden_width
    )
    outgoing = jnp.repeat(picked, copies, axis=0)
    arrived = lax.all_to_all(outgoing, "ctx", split_axis=0, concat_axis=2, tiled=True)
    coef_table = merge_coef[source_order].reshape(MERGED // per_lane, per_lane, 2)
    pair_coef = lax.dynamic_index_in_dim(coef_table, lane_group, 0, keepdims=False)
    lane_weights = (
        pair_coef[:, 0, None, None] * arrived[:, 0].astype(jnp.float32)
        + pair_coef[:, 1, None, None] * arrived[:, 1].astype(jnp.float32)
    ).astype(jnp.bfloat16)
    recv_hidden, recv_grad, recv_member = (
        lax.all_to_all(send_hidden, "ctx", split_axis=0, concat_axis=0, tiled=True),
        lax.all_to_all(send_grad, "ctx", split_axis=0, concat_axis=0, tiled=True),
        lax.all_to_all(send_member, "ctx", split_axis=0, concat_axis=0, tiled=True),
    )
    out_rows, back_rows, lane_grads = expert_rows(
        recv_hidden.reshape(-1, hidden_width),
        recv_grad.reshape(-1, out_width),
        recv_member.reshape(-1),
        lane_weights,
    )
    home_out, home_back = (
        lax.all_to_all(
            out_rows.astype(jnp.bfloat16).reshape(ctx_count, capacity, out_width),
            "ctx",
            split_axis=0,
            concat_axis=0,
            tiled=True,
        ),
        lax.all_to_all(
            back_rows.astype(jnp.bfloat16).reshape(ctx_count, capacity, hidden_width),
            "ctx",
            split_axis=0,
            concat_axis=0,
            tiled=True,
        ),
    )
    slot_out = jnp.concatenate(
        [home_out.reshape(-1, out_width), jnp.zeros((1, out_width), jnp.bfloat16)], axis=0
    )[slot_index].reshape(tok_count, top_count, out_width)
    hidden_grad = jnp.concatenate(
        [home_back.reshape(-1, hidden_width), jnp.zeros((1, hidden_width), jnp.bfloat16)], axis=0
    )[slot_index].reshape(1, tok_count, top_count, hidden_width)
    mixed = (
        jnp.sum(gate_probs[:, :, None] * slot_out.astype(jnp.float32), axis=1)
        .astype(jnp.bfloat16)
        .reshape(1, tok_count, out_width)
    )
    score_grad = jnp.einsum(
        "td,tkd->tk",
        out_grad.reshape(tok_count, out_width),
        slot_out,
        preferred_element_type=jnp.float32,
    )
    chosen_grad = gate_probs * (
        score_grad - jnp.sum(gate_probs * score_grad, axis=1, keepdims=True)
    )
    logit_grad = jnp.sum(pick_float * chosen_grad[:, :, None], axis=1)
    logit_half = logit_grad.astype(jnp.bfloat16)
    token_grad = (
        lax.dot_general(
            logit_half, router_w, (((1,), (1,)), ((), ())), preferred_element_type=jnp.float32
        )
        .astype(jnp.bfloat16)
        .reshape(1, tok_count, feature_count)
    )
    part_router_w = lax.dot_general(
        flat_x, logit_half, (((0,), (0,)), ((), ())), preferred_element_type=jnp.float32
    )
    part_router_b = jnp.sum(logit_grad, axis=0)
    arrived_grads = lax.all_to_all(
        lane_grads.reshape(per_lane, ctx_count, row_share, hidden_width),
        "ctx",
        split_axis=1,
        concat_axis=0,
        tiled=True,
    )
    merged_grad = (
        arrived_grads.reshape(MERGED // per_lane, copies, per_lane, row_share, hidden_width)
        .sum(axis=1)
        .reshape(MERGED, row_share, hidden_width)
    )
    source_grad = merged_grad[merge_map]
    coef_part = jnp.einsum(
        "edf,edf->e", source_grad, source_w.astype(jnp.float32), precision=lax.Precision.HIGHEST
    )
    summed = lax.psum_scatter(
        source_grad * merge_coef[:, None, None], "rep", scatter_dimension=2, tiled=True
    )
    source_w_grad = summed * grad_scale
    router_sum, bias_sum, coef_sum = lax.psum(
        (part_router_w, part_router_b, coef_part), ("ctx", "rep")
    )
    return (
        mixed,
        hidden_grad,
        token_grad,
        router_sum * grad_scale,
        bias_sum * grad_scale,
        coef_sum * grad_scale,
        source_w_grad,
    )


def solution(mesh):
    in_specs = (
        P("rep", "ctx", None),
        P(),
        P(),
        P("rep", "ctx", None, None),
        P("rep", "ctx", None),
        P(),
        P(),
        P(None, "ctx", None),
        P("rep", "ctx", None),
    )
    out_specs = (
        P("rep", "ctx", None),
        P("rep", "ctx", None, None),
        P("rep", "ctx", None),
        P(),
        P(),
        P(),
        P(None, "ctx", "rep"),
    )
    return jax.shard_map(
        on_device, mesh=mesh, in_specs=in_specs, out_specs=out_specs, check_vma=False
    )
```

profile of v0, /device:TPU:1, one launch (start us, length us, event | category | flops | bytes accessed | tf_op | source)
XLA Modules:
  0.0 1014.5 jit_solution(12828136133311541424)
XLA Ops:
  11.4 2.4 scatter_custom_fusion
  13.9 2.8 gather_fusion
  17.5 13.5 %all-to-all-start = ((s32[64,1,10]{2,1,0:T(1,128)}), s32[64,1,10]{2,1,0:T(1,128)S(1)}, u32[]{:S(2)}, u32[]{:S(2)}) async-start(s32[64,1,10]{2,1,0:T(1,128)} %bitcast.5), calls=%async_computation | async-start | bytes 65536 | tf_op jit(solution)/shard_map/all_to_all | solution.py:110
  33.8 3.7 gather_fusion.1
  37.5 4.2 reshape.274
  41.7 11.1 %all-to-all-start.1 = ((bf16[64,10,1536]{2,1,0:T(8,128)(2,1)}), bf16[64,10,1536]{2,1,0:T(8,128)(2,1)}, u32[]{:S(2)}, u32[]{:S(2)}) async-start(bf16[64,10,1536]{2,1,0:T(8,128)(2,1)} %reshape.274), calls=%async_computation.1 | async-start | bytes 6291456 | tf_op jit(solution)/shard_map/all_to_all | solution.py:108
  53.7 2.1 gather_fusion.3
  55.8 66.0 %all-to-all-done.1 = bf16[64,10,1536]{2,1,0:T(8,128)(2,1)} async-done(((bf16[64,10,1536]{2,1,0:T(8,128)(2,1)}), bf16[64,10,1536]{2,1,0:T(8,128)(2,1)}, u32[]{:S(2)}, u32[]{:S(2)}) %all-to-all-start.1) | async-done | bytes 1966112 | tf_op jit(solution)/shard_map/all_to_all | solution.py:108
  121.8 6.5 broadcast_in_dim.85
  128.3 10.5 %all-to-all-start.2 = ((bf16[64,2,24,1536]{3,2,1,0:T(8,128)(2,1)}), bf16[64,2,24,1536]{3,2,1,0:T(8,128)(2,1)}, u32[]{:S(2)}, u32[]{:S(2)}) async-start(bf16[64,2,24,1536]{3,2,1,0:T(8,128)(2,1)} %bitcast.77), calls=%async_computation.2 | async-start | bytes 18874368 | tf_op jit(solution)/shard_map/all_to_all | solution.py:100
  140.5 2.9 reshape.275
  143.4 199.7 %all-to-all-done.2 = bf16[64,2,24,1536]{3,2,1,0:T(8,128)(2,1)} async-done(((bf16[64,2,24,1536]{3,2,1,0:T(8,128)(2,1)}), bf16[64,2,24,1536]{3,2,1,0:T(8,128)(2,1)}, u32[]{:S(2)}, u32[]{:S(2)}) %all-to-all-start.2) | async-done | bytes 9437216 | tf_op jit(solution)/shard_map/all_to_all | solution.py:100
  343.1 8.1 copy.44
  351.1 9.8 select_convert_fusion.1
  360.9 4.2 reshape.279
  365.1 11.4 %all-to-all-start.3 = ((bf16[64,10,1536]{2,1,0:T(8,128)(2,1)}), bf16[64,10,1536]{2,1,0:T(8,128)(2,1)}, u32[]{:S(2)}, u32[]{:S(2)}) async-start(bf16[64,10,1536]{2,1,0:T(8,128)(2,1)} %reshape.279), calls=%async_computation.3 | async-start | bytes 6291456 | tf_op jit(solution)/shard_map/all_to_all | solution.py:119
  376.7 2.2 mul.170
  378.9 5.0 mul.171
  384.2 61.5 %all-to-all-done.3 = bf16[64,10,1536]{2,1,0:T(8,128)(2,1)} async-done(((bf16[64,10,1536]{2,1,0:T(8,128)(2,1)}), bf16[64,10,1536]{2,1,0:T(8,128)(2,1)}, u32[]{:S(2)}, u32[]{:S(2)}) %all-to-all-start.3) | async-done | bytes 1966112 | tf_op jit(solution)/shard_map/all_to_all | solution.py:119
  445.7 4.3 reshape.280
  451.6 2.9 gather_fusion.4
  454.6 2.9 reshape.281
  457.5 1.8 fusion.2
  459.7 2.1 multiply_convert_fusion
  461.9 3.7 gather_fusion.5
  465.7 4.2 reshape.283
  469.9 11.0 %all-to-all-start.4 = ((bf16[64,10,1536]{2,1,0:T(8,128)(2,1)}), bf16[64,10,1536]{2,1,0:T(8,128)(2,1)}, u32[]{:S(2)}, u32[]{:S(2)}) async-start(bf16[64,10,1536]{2,1,0:T(8,128)(2,1)} %reshape.283), calls=%async_computation.4 | async-start | bytes 6291456 | tf_op jit(solution)/shard_map/all_to_all | solution.py:109
  480.8 4.2 reshape.380
  485.1 64.7 %all-to-all-done.4 = bf16[64,10,1536]{2,1,0:T(8,128)(2,1)} async-done(((bf16[64,10,1536]{2,1,0:T(8,128)(2,1)}), bf16[64,10,1536]{2,1,0:T(8,128)(2,1)}, u32[]{:S(2)}, u32[]{:S(2)}) %all-to-all-start.4) | async-done | bytes 1966112 | tf_op jit(solution)/shard_map/all_to_all | solution.py:109
  549.8 2.9 reshape.284
  554.5 4.0 copy.46
  558.4 9.7 convolution_bitcast_fusion
  568.1 10.7 %all-to-all-start.6 = ((f32[1,64,24,1536]{3,2,0,1:T(8,128)}), f32[1,64,24,1536]{3,2,0,1:T(8,128)}, u32[]{:S(2)}, u32[]{:S(2)}) async-start(f32[1,64,24,1536]{3,2,0,1:T(8,128)} %convolution_bitcast_fusion), calls=%async_computation.6 | async-start | bytes 18874368 | tf_op jit(solution)/shard_map/all_to_all | solution.py:167
  580.2 205.3 %all-to-all-done.6 = f32[1,64,24,1536]{3,2,0,1:T(8,128)} async-done(((f32[1,64,24,1536]{3,2,0,1:T(8,128)}), f32[1,64,24,1536]{3,2,0,1:T(8,128)}, u32[]{:S(2)}, u32[]{:S(2)}) %all-to-all-start.6) | async-done | bytes 9437216 | tf_op jit(solution)/shard_map/all_to_all | solution.py:167
  785.5 5.2 reduce_sum.102
  790.7 3.1 gather_fusion.7
  793.8 6.3 broadcast_multiply_fusion
  801.6 9.6 select_convert_fusion
  811.3 4.2 reshape.285
  815.5 12.3 %all-to-all-start.5 = ((bf16[64,10,1536]{2,1,0:T(8,128)(2,1)}), bf16[64,10,1536]{2,1,0:T(8,128)(2,1)}, u32[]{:S(2)}, u32[]{:S(2)}) async-start(bf16[64,10,1536]{2,1,0:T(8,128)(2,1)} %reshape.285), calls=%async_computation.5 | async-start | bytes 6291456 | tf_op jit(solution)/shard_map/all_to_all | solution.py:126
  829.1 3.1 multiply_reduce_fusion.1
  832.1 81.9 %all-reduce.7.cloned.1.call-done = f32[2880,32]{0,1:T(8,128)} async-done(((f32[2880,32]{0,1:T(8,128)}), f32[2880,32]{0,1:T(8,128)}) %all-reduce.7.cloned.1.call-update) | async-done | bytes 368656 | tf_op jit(solution)/shard_map/psum | solution.py:187
  914.0 1.8 broadcast_multiply_fusion.2
  915.8 4.2 reshape.286
  921.7 3.0 gather_fusion.6
  924.7 3.8 reshape.287
  928.5 75.4 %all-reduce.4 = (f32[32]{0:T(128)S(1)}, f32[32]{0:T(128)S(1)}) all-reduce(f32[32]{0:T(128)S(1)} %get-tuple-element.7, f32[32]{0:T(128)S(1)} %get-tuple-element.16), channel_id=1, replica_groups=mesh['ctx'=64,'rep'=4] {'ctx','rep'}, use_global_device_ids=true, to_apply=%region_14.15 | all-reduce | flops 64 | bytes 512 | tf_op jit(solution)/shard_map/psum | solution.py:187
  1004.4 2.4 broadcast_multiply_fusion.1
  (93 shorter events, 20.1 us)
Async XLA Ops:
  8.0 375.8 %copy-start = (bf16[1,128,2880]{1,2,0:T(8,128)(2,1)S(1)}, bf16[1,128,2880]{1,2,0:T(8,128)(2,1)}, u32[]{:S(2)}) copy-start(bf16[1,128,2880]{1,2,0:T(8,128)(2,1)} %param.9) | copy-start | bytes 2211844
  10.8 20.2 %copy-start.7 = (bf16[1,128,4,1536]{3,2,1,0:T(4,128)(2,1)S(1)}, bf16[1,128,4,1536]{3,2,1,0:T(4,128)(2,1)}, u32[]{:S(2)}) copy-start(bf16[1,128,4,1536]{3,2,1,0:T(4,128)(2,1)} %param.12) | copy-start | bytes 4718596
  17.5 24.2 %all-to-all-start = ((s32[64,1,10]{2,1,0:T(1,128)}), s32[64,1,10]{2,1,0:T(1,128)S(1)}, u32[]{:S(2)}, u32[]{:S(2)}) async-start(s32[64,1,10]{2,1,0:T(1,128)} %bitcast.5), calls=%async_computation | async-start | bytes 65536 | tf_op jit(solution)/shard_map/all_to_all | solution.py:110
  41.7 11.1 %copy-start.12 = (s32[32]{0:T(128)S(1)}, s32[32]{0:T(128)}, u32[]{:S(2)}) copy-start(s32[32]{0:T(128)} %param.14) | copy-start | bytes 388
  41.7 12.0 %copy-start.2 = (bf16[32,24,1536]{2,1,0:T(8,128)(2,1)S(1)}, bf16[32,24,1536]{2,1,0:T(8,128)(2,1)}, u32[]{:S(2)}) copy-start(bf16[32,24,1536]{2,1,0:T(8,128)(2,1)} %param.16) | copy-start | bytes 7077892
  41.7 80.1 %all-to-all-start.1 = ((bf16[64,10,1536]{2,1,0:T(8,128)(2,1)}), bf16[64,10,1536]{2,1,0:T(8,128)(2,1)}, u32[]{:S(2)}, u32[]{:S(2)}) async-start(bf16[64,10,1536]{2,1,0:T(8,128)(2,1)} %reshape.274), calls=%async_computation.1 | async-start | bytes 6291456 | tf_op jit(solution)/shard_map/all_to_all | solution.py:108
  128.3 10.5 %copy-start.1 = (f32[32]{0:T(128)S(1)}, f32[32]{0:T(128)}, u32[]{:S(2)}) copy-start(f32[32]{0:T(128)} %param.15) | copy-start | bytes 388
  128.3 214.8 %all-to-all-start.2 = ((bf16[64,2,24,1536]{3,2,1,0:T(8,128)(2,1)}), bf16[64,2,24,1536]{3,2,1,0:T(8,128)(2,1)}, u32[]{:S(2)}, u32[]{:S(2)}) async-start(bf16[64,2,24,1536]{3,2,1,0:T(8,128)(2,1)} %bitcast.77), calls=%async_computation.2 | async-start | bytes 18874368 | tf_op jit(solution)/shard_map/all_to_all | solution.py:100
  365.1 11.4 %copy-start.9 = (bf16[1,128,1536]{2,1,0:T(8,128)(2,1)S(1)}, bf16[1,128,1536]{2,1,0:T(8,128)(2,1)}, u32[]{:S(2)}) copy-start(bf16[1,128,1536]{2,1,0:T(8,128)(2,1)} %param.17) | copy-start | bytes 1179652
  365.1 80.5 %all-to-all-start.3 = ((bf16[64,10,1536]{2,1,0:T(8,128)(2,1)}), bf16[64,10,1536]{2,1,0:T(8,128)(2,1)}, u32[]{:S(2)}, u32[]{:S(2)}) async-start(bf16[64,10,1536]{2,1,0:T(8,128)(2,1)} %reshape.279), calls=%async_computation.3 | async-start | bytes 6291456 | tf_op jit(solution)/shard_map/all_to_all | solution.py:119
  378.9 5.0 copy-start.8
  378.9 5.0 copy-start.13
  378.9 5.2 copy-start.11
  454.6 3.0 copy-start.10
  457.5 1.8 copy-start.5
  469.9 80.0 %all-to-all-start.4 = ((bf16[64,10,1536]{2,1,0:T(8,128)(2,1)}), bf16[64,10,1536]{2,1,0:T(8,128)(2,1)}, u32[]{:S(2)}, u32[]{:S(2)}) async-start(bf16[64,10,1536]{2,1,0:T(8,128)(2,1)} %reshape.283), calls=%async_computation.4 | async-start | bytes 6291456 | tf_op jit(solution)/shard_map/all_to_all | solution.py:109
  552.7 5.7 copy-start.3
  568.1 217.4 %all-to-all-start.6 = ((f32[1,64,24,1536]{3,2,0,1:T(8,128)}), f32[1,64,24,1536]{3,2,0,1:T(8,128)}, u32[]{:S(2)}, u32[]{:S(2)}) async-start(f32[1,64,24,1536]{3,2,0,1:T(8,128)} %convolution_bitcast_fusion), calls=%async_computation.6 | async-start | bytes 18874368 | tf_op jit(solution)/shard_map/all_to_all | solution.py:167
  578.9 335.2 %all-reduce.7.cloned.1.call-start = ((), (), s32[]{:S(2)}) async-start(), calls=%async_computation.8 | async-start | bytes 753664 | tf_op jit(solution)/shard_map/psum | solution.py:187
  580.2 424.2 %reduce-scatter.2.cloned.1.call-start = ((), (), s32[]{:S(2)}) async-start(), calls=%async_computation.9 | async-start | bytes 5898240 | tf_op jit(solution)/shard_map/reduce_scatter | solution.py:183
  800.1 1.5 copy-start.4
  815.5 13.6 %copy-start.6 = (bf16[128,4,1536]{2,1,0:T(4,128)(2,1)S(1)}, bf16[128,4,1536]{2,1,0:T(4,128)(2,1)}, u32[]{:S(2)}) copy-start(bf16[128,4,1536]{2,1,0:T(4,128)(2,1)} %copy-done.5) | copy-start | bytes 4718596
  815.5 100.3 %all-to-all-start.5 = ((bf16[64,10,1536]{2,1,0:T(8,128)(2,1)}), bf16[64,10,1536]{2,1,0:T(8,128)(2,1)}, u32[]{:S(2)}, u32[]{:S(2)}) async-start(bf16[64,10,1536]{2,1,0:T(8,128)(2,1)} %reshape.285), calls=%async_computation.5 | async-start | bytes 6291456 | tf_op jit(solution)/shard_map/all_to_all | solution.py:126
Sparse Core Ops, SparseCore 0:
  585.8 328.2 all-reduce.6
Sparse Core Ops, SparseCore 1:
  800.2 83.5 reduce-scatter.1
where the time goes:
time: 1020 us; the launch traced here: 1010 us
  waiting for transfers between devices  679 us (67%)
  local copies, waits for them, and re-layouts  104 us (10%)
  starting transfers between devices  80.5 us (8%)
  blocking collectives  75.4 us (7%)
  matrix products  33.5 us (3%)
  other arithmetic  25.9 us (3%)
  between operations  16.1 us (2%)
    all_to_all x1, waiting for transfers between devices, on_device(): lax.all_to_all(lane_grads.reshape(per_lane, ctx_count, row_share, hidden_...  205 us
    all_to_all x1, waiting for transfers between devices, on_device(): lax.all_to_all(outgoing, 'ctx', split_axis=0, concat_axis=2, tiled=True)  200 us
    psum x1, waiting for transfers between devices, on_device(): lax.psum((part_router_w, part_router_b, coef_part), ('ctx', 'rep'))  81.9 us
    psum x1, blocking collectives, on_device(): lax.psum((part_router_w, part_router_b, coef_part), ('ctx', 'rep'))  75.4 us
    all_to_all x1, waiting for transfers between devices, on_device(): lax.all_to_all(send_hidden, 'ctx', split_axis=0, concat_axis=0, tiled=True)  66 us
    all_to_all x1, waiting for transfers between devices, on_device(): lax.all_to_all(send_grad, 'ctx', split_axis=0, concat_axis=0, tiled=True)  64.7 us
    all_to_all x1, waiting for transfers between devices, on_device(): lax.all_to_all(out_rows.astype(jnp.bfloat16).reshape(ctx_count, capacity,...  61.5 us
  transfers between devices with their start and end apart: 9, of which 6 were waited for; matrix products, arithmetic and copies ran while one was open for 8% of the time, Pallas kernels for 0%

commit v1 on v0

--- a/solution.py
+++ b/solution.py
@@ -1,3 +1,4 @@
+import functools
 import math
 import jax
 import jax.numpy as jnp
@@ -5,6 +6,14 @@
 from jax.sharding import PartitionSpec as P
 
 MERGED = 16
+
+
+def switch_the_hubs(inputs, comm_axis, ax_name):
+    heard = lax.psum(lax.psum(inputs, axis_name=comm_axis), axis_name=ax_name)
+    return heard
+
+
+_number_panel = functools.partial(switch_the_hubs, comm_axis="rep", ax_name="ctx")
 
 
 def expert_rows(rows_hidden, rows_grad, rows_member, lane_weights):
@@ -184,9 +193,7 @@
         source_grad * merge_coef[:, None, None], "rep", scatter_dimension=2, tiled=True
     )
     source_w_grad = summed * grad_scale
-    router_sum, bias_sum, coef_sum = lax.psum(
-        (part_router_w, part_router_b, coef_part), ("ctx", "rep")
-    )
+    router_sum, bias_sum, coef_sum = _number_panel((part_router_w, part_router_b, coef_part))
     return (
         mixed,
         hidden_grad,

time: 1020 us -> 1430 us (1.40)
  the two profiles are of different devices: /device:TPU:1 before, /device:TPU:16 now
where the time goes in v1:
time: 1430 us; the launch traced here: 1420 us
  waiting for transfers between devices  1020 us (71%)
  blocking collectives  163 us (11%)
  local copies, waits for them, and re-layouts  104 us (7%)
  starting transfers between devices  60.6 us (4%)
  matrix products  33.5 us (2%)
  other arithmetic  25.9 us (2%)
  between operations  14.4 us (1%)
    psum x2, waiting for transfers between devices, switch_the_hubs(): heard = lax.psum(lax.psum(inputs, axis_name=comm_axis), axis_name=ax_name)  461 us
    all_to_all x1, waiting for transfers between devices, on_device(): lax.all_to_all(outgoing, 'ctx', split_axis=0, concat_axis=2, tiled=True)  202 us
    psum x2, blocking collectives, switch_the_hubs(): heard = lax.psum(lax.psum(inputs, axis_name=comm_axis), axis_name=ax_name)  163 us
    all_to_all x1, waiting for transfers between devices, on_device(): lax.all_to_all(lane_grads.reshape(per_lane, ctx_count, row_share, hidden_...  149 us
    all_to_all x1, waiting for transfers between devices, on_device(): lax.all_to_all(send_hidden, 'ctx', split_axis=0, concat_axis=0, tiled=True)  69.9 us
    all_to_all x1, waiting for transfers between devices, on_device(): lax.all_to_all(send_grad, 'ctx', split_axis=0, concat_axis=0, tiled=True)  69.8 us
    all_to_all x1, waiting for transfers between devices, on_device(): lax.all_to_all(out_rows.astype(jnp.bfloat16).reshape(ctx_count, capacity,...  66.8 us
  transfers between devices with their start and end apart: 10, of which 7 were waited for; matrix products, arithmetic and copies ran while one was open for 6% of the time, Pallas kernels for 0%

profile of v1, /device:TPU:16, one launch (start us, length us, event | category | flops | bytes accessed | tf_op | source)
XLA Modules:
  0.0 1420.1 jit_solution(617011797049860384)
XLA Ops:
  10.6 2.4 scatter_custom_fusion
  13.1 2.8 gather_fusion
  16.6 12.7 all-to-all-start
  32.2 3.7 gather_fusion.1
  35.9 4.2 reshape.274
  40.0 11.6 all-to-all-start.1
  52.6 2.1 gather_fusion.3
  54.7 69.9 %all-to-all-done.1 = bf16[64,10,1536]{2,1,0:T(8,128)(2,1)} async-done(((bf16[64,10,1536]{2,1,0:T(8,128)(2,1)}), bf16[64,10,1536]{2,1,0:T(8,128)(2,1)}, u32[]{:S(2)}, u32[]{:S(2)}) %all-to-all-start.1) | async-done | bytes 1966112 | tf_op jit(solution)/shard_map/all_to_all | solution.py:117
  124.6 6.5 broadcast_in_dim.85
  131.1 7.1 all-to-all-start.2
  139.9 2.9 reshape.275
  142.8 202.0 %all-to-all-done.2 = bf16[64,2,24,1536]{3,2,1,0:T(8,128)(2,1)} async-done(((bf16[64,2,24,1536]{3,2,1,0:T(8,128)(2,1)}), bf16[64,2,24,1536]{3,2,1,0:T(8,128)(2,1)}, u32[]{:S(2)}, u32[]{:S(2)}) %all-to-all-start.2) | async-done | bytes 9437216 | tf_op jit(solution)/shard_map/all_to_all | solution.py:109
  344.8 8.1 copy.44
  352.9 9.8 select_convert_fusion.1
  362.6 4.2 reshape.279
  366.9 7.9 all-to-all-start.3
  374.9 2.2 mul.170
  377.1 5.0 mul.171
  382.4 66.8 %all-to-all-done.3 = bf16[64,10,1536]{2,1,0:T(8,128)(2,1)} async-done(((bf16[64,10,1536]{2,1,0:T(8,128)(2,1)}), bf16[64,10,1536]{2,1,0:T(8,128)(2,1)}, u32[]{:S(2)}, u32[]{:S(2)}) %all-to-all-start.3) | async-done | bytes 1966112 | tf_op jit(solution)/shard_map/all_to_all | solution.py:128
  449.2 4.3 reshape.280
  455.1 2.9 gather_fusion.4
  458.1 2.9 reshape.281
  463.2 2.1 multiply_convert_fusion
  465.5 3.7 gather_fusion.5
  469.2 4.2 reshape.283
  473.4 5.9 all-to-all-start.4
  479.3 4.2 reshape.380
  483.5 69.8 %all-to-all-done.4 = bf16[64,10,1536]{2,1,0:T(8,128)(2,1)} async-done(((bf16[64,10,1536]{2,1,0:T(8,128)(2,1)}), bf16[64,10,1536]{2,1,0:T(8,128)(2,1)}, u32[]{:S(2)}, u32[]{:S(2)}) %all-to-all-start.4) | async-done | bytes 1966112 | tf_op jit(solution)/shard_map/all_to_all | solution.py:118
  553.3 2.9 reshape.284
  558.0 4.0 copy.46
  562.0 9.7 convolution_bitcast_fusion
  571.6 5.9 all-to-all-start.6
  578.9 58.4 %all-reduce.9.cloned.1.call-done = f32[2880,32]{0,1:T(8,128)} async-done(((f32[2880,32]{0,1:T(8,128)}), f32[2880,32]{0,1:T(8,128)}) %all-reduce.9.cloned.1.call-update) | async-done | bytes 368656 | tf_op jit(solution)/shard_map/psum | solution.py:12
  637.3 149.4 %all-to-all-done.6 = f32[1,64,24,1536]{3,2,0,1:T(8,128)} async-done(((f32[1,64,24,1536]{3,2,0,1:T(8,128)}), f32[1,64,24,1536]{3,2,0,1:T(8,128)}, u32[]{:S(2)}, u32[]{:S(2)}) %all-to-all-start.6) | async-done | bytes 9437216 | tf_op jit(solution)/shard_map/all_to_all | solution.py:176
  786.7 5.2 reduce_sum.102
  791.9 3.1 gather_fusion.7
  795.0 6.3 broadcast_multiply_fusion
  802.8 9.7 select_convert_fusion
  812.5 4.2 reshape.285
  816.7 9.4 all-to-all-start.5
  827.4 3.1 multiply_reduce_fusion.1
  830.4 402.5 %all-reduce.11.cloned.1.call-done = f32[2880,32]{0,1:T(8,128)} async-done(((f32[2880,32]{0,1:T(8,128)}), f32[2880,32]{0,1:T(8,128)}) %all-reduce.11.cloned.1.call-update) | async-done | bytes 368656 | tf_op jit(solution)/shard_map/psum | solution.py:12
  1234.7 4.2 reshape.286
  1240.7 3.0 gather_fusion.6
  1243.6 4.2 reshape.287
  1247.8 7.1 all-reduce.5
  1254.9 155.5 %all-reduce.4 = (f32[32]{0:T(128)S(1)}, f32[32]{0:T(128)S(1)}) all-reduce(f32[32]{0:T(128)S(1)} %get-tuple-element.11, f32[32]{0:T(128)S(1)} %get-tuple-element.12), channel_id=1, replica_groups=mesh['ctx'=64,'rep'=4] {'ctx'}, use_global_device_ids=true, to_apply=%region_16.17 | all-reduce | flops 64 | bytes 512 | tf_op jit(solution)/shard_map/psum | solution.py:12
  1410.9 2.4 broadcast_multiply_fusion.1
  (97 shorter events, 23.7 us)
Async XLA Ops:
  7.2 374.9 %copy-start = (bf16[1,128,2880]{1,2,0:T(8,128)(2,1)S(1)}, bf16[1,128,2880]{1,2,0:T(8,128)(2,1)}, u32[]{:S(2)}) copy-start(bf16[1,128,2880]{1,2,0:T(8,128)(2,1)} %param.9) | copy-start | bytes 2211844
  10.0 19.4 %copy-start.7 = (bf16[1,128,4,1536]{3,2,1,0:T(4,128)(2,1)S(1)}, bf16[1,128,4,1536]{3,2,1,0:T(4,128)(2,1)}, u32[]{:S(2)}) copy-start(bf16[1,128,4,1536]{3,2,1,0:T(4,128)(2,1)} %param.12) | copy-start | bytes 4718596
  16.6 23.4 %all-to-all-start = ((s32[64,1,10]{2,1,0:T(1,128)}), s32[64,1,10]{2,1,0:T(1,128)S(1)}, u32[]{:S(2)}, u32[]{:S(2)}) async-start(s32[64,1,10]{2,1,0:T(1,128)} %bitcast.5), calls=%async_computation | async-start | bytes 65536 | tf_op jit(solution)/shard_map/all_to_all | solution.py:119
  40.0 11.6 copy-start.12
  40.0 12.6 copy-start.2
  40.0 84.6 %all-to-all-start.1 = ((bf16[64,10,1536]{2,1,0:T(8,128)(2,1)}), bf16[64,10,1536]{2,1,0:T(8,128)(2,1)}, u32[]{:S(2)}, u32[]{:S(2)}) async-start(bf16[64,10,1536]{2,1,0:T(8,128)(2,1)} %reshape.274), calls=%async_computation.1 | async-start | bytes 6291456 | tf_op jit(solution)/shard_map/all_to_all | solution.py:117
  131.1 7.1 copy-start.1
  131.1 213.7 %all-to-all-start.2 = ((bf16[64,2,24,1536]{3,2,1,0:T(8,128)(2,1)}), bf16[64,2,24,1536]{3,2,1,0:T(8,128)(2,1)}, u32[]{:S(2)}, u32[]{:S(2)}) async-start(bf16[64,2,24,1536]{3,2,1,0:T(8,128)(2,1)} %bitcast.77), calls=%async_computation.2 | async-start | bytes 18874368 | tf_op jit(solution)/shard_map/all_to_all | solution.py:109
  366.9 8.0 copy-start.9
  366.9 82.3 %all-to-all-start.3 = ((bf16[64,10,1536]{2,1,0:T(8,128)(2,1)}), bf16[64,10,1536]{2,1,0:T(8,128)(2,1)}, u32[]{:S(2)}, u32[]{:S(2)}) async-start(bf16[64,10,1536]{2,1,0:T(8,128)(2,1)} %reshape.279), calls=%async_computation.3 | async-start | bytes 6291456 | tf_op jit(solution)/shard_map/all_to_all | solution.py:128
  377.1 5.0 copy-start.8
  377.1 5.0 copy-start.13
  377.1 5.2 copy-start.11
  458.1 3.0 copy-start.10
  461.0 1.8 copy-start.5
  473.4 80.0 %all-to-all-start.4 = ((bf16[64,10,1536]{2,1,0:T(8,128)(2,1)}), bf16[64,10,1536]{2,1,0:T(8,128)(2,1)}, u32[]{:S(2)}, u32[]{:S(2)}) async-start(bf16[64,10,1536]{2,1,0:T(8,128)(2,1)} %reshape.283), calls=%async_computation.4 | async-start | bytes 6291456 | tf_op jit(solution)/shard_map/all_to_all | solution.py:118
  556.3 5.7 copy-start.3
  571.6 215.1 %all-to-all-start.6 = ((f32[1,64,24,1536]{3,2,0,1:T(8,128)}), f32[1,64,24,1536]{3,2,0,1:T(8,128)}, u32[]{:S(2)}, u32[]{:S(2)}) async-start(f32[1,64,24,1536]{3,2,0,1:T(8,128)} %convolution_bitcast_fusion), calls=%async_computation.6 | async-start | bytes 18874368 | tf_op jit(solution)/shard_map/all_to_all | solution.py:176
  577.5 59.8 %all-reduce.9.cloned.1.call-start = ((), (), s32[]{:S(2)}) async-start(), calls=%async_computation.8 | async-start | bytes 753664 | tf_op jit(solution)/shard_map/psum | solution.py:12
  578.8 654.2 %all-reduce.11.cloned.1.call-start = ((), (), s32[]{:S(2)}) async-start(), calls=%async_computation.9 | async-start | bytes 753664 | tf_op jit(solution)/shard_map/psum | solution.py:12
  637.3 773.7 %reduce-scatter.2.cloned.1.call-start = ((), (), s32[]{:S(2)}) async-start(), calls=%async_computation.10 | async-start | bytes 5898240 | tf_op jit(solution)/shard_map/reduce_scatter | solution.py:192
  801.3 1.5 copy-start.4
  816.7 10.7 copy-start.6
  816.7 418.0 %all-to-all-start.5 = ((bf16[64,10,1536]{2,1,0:T(8,128)(2,1)}), bf16[64,10,1536]{2,1,0:T(8,128)(2,1)}, u32[]{:S(2)}, u32[]{:S(2)}) async-start(bf16[64,10,1536]{2,1,0:T(8,128)(2,1)} %reshape.285), calls=%async_computation.5 | async-start | bytes 6291456 | tf_op jit(solution)/shard_map/all_to_all | solution.py:135
Sparse Core Ops, SparseCore 0:
  581.5 55.6 all-reduce.8
  639.9 593.0 all-reduce.10
  1235.8 53.1 reduce-scatter.1
